TPU v7x, 256 devices: a whole 4x4x8 slice. The times are simulated.
256 devices in a mesh: doc: 64 (over z, y, core), tp: 4 (over x).
Axes of the slice: x: 4, y: 4, z: 8, core: 2. Of those that a mesh axis runs over, the one named last changes fastest.
Arguments:
- storage: bfloat16 [32768, 3584], P('doc', 'tp'), may hold values from -40 to 40
- row_doc: int32 [32768], P('doc'), may hold values from -1 to 63, as said below
- row_pos: int32 [32768], P('doc'), may hold values from -1 to 511, as said below
- doc_len: int32 [64], replicated, may hold values from 64 to 512, as said below
- partner: int32 [64], replicated, may hold values from 0 to 63, as said below
- norm_gain: bfloat16 [3584], replicated, may hold values from 0.25 to 1.75
- qkv_weight: bfloat16 [3584, 4608], P('doc', 'tp'), may hold values from -0.09375 to 0.09375
- qkv_bias: bfloat16 [4608], P('tp'), may hold values from -24 to 24
Outputs:
- attention: bfloat16 [65536, 3584], P('doc', 'tp')
Inputs may be any that keep to these rules, and one draw needn't show every extreme that they name: `row_doc`: the rows 0 to doc_len[d] - 1 of each document d are stored exactly once over all devices, one to a slot; -1 marks an empty slot. One device stores at most 8 rows of any one document, and exactly 8 rows of a document of 512 tokens. `row_pos`: -1 for an empty slot. `doc_len`: some document has 512 tokens and some has 64. partner[partner[d]] = d and partner[d] != d.
All inputs are finite; a program needn't handle non-finite values.
Results may differ from a plain program's by a relative error of at most 0.008.
The roundings to bfloat16 on the way count: a program that leaves them out, or rounds other values in their place, can miss the bound.
Values may be sent and summed in bfloat16 or wider, within the bound.
A program may use at most 64 MiB of HBM per device.

v0:
```python
import jax
import jax.numpy as jnp
from jax import lax
from jax.sharding import PartitionSpec as P

HEADS = 28
KVH = 4
HD = 128
HALF = 512
ROPE_BASE = 1000000.0
EPSILON = 1e-06
BLOCK_ROWS = 512


def from_partner(value, axis, stride):
    mask = 2**stride
    pairs = [(source, source ^ mask) for source in range(lax.axis_size(axis))]
    return lax.ppermute(value, axis, pairs)


def pairing(partner):
    doc_ids = jnp.arange(partner.shape[0], dtype=jnp.int32)
    first_flag = (doc_ids < partner).astype(jnp.int32)
    before = jnp.cumsum(first_flag) - first_flag
    low_doc = jnp.minimum(doc_ids, partner)
    pick_mask = (low_doc[:, None] == doc_ids[None, :]).astype(jnp.int32)
    pair_index = jnp.sum(pick_mask * before[None, :], axis=1)
    scorer = 2 * pair_index + 1 - first_flag
    match_mask = (scorer[None, :] == doc_ids[:, None]).astype(jnp.int32)
    own_doc = jnp.sum(match_mask * doc_ids[None, :], axis=1)
    return (scorer, own_doc)


def rope_tables(length, head_dim):
    half_dim = head_dim // 2
    freq_ids = jnp.arange(half_dim, dtype=jnp.float32)
    inv_freq = jnp.exp(-(2.0 * freq_ids / head_dim) * jnp.log(jnp.float32(ROPE_BASE)))
    angles = jnp.arange(length, dtype=jnp.float32)[:, None] * inv_freq[None, :]
    cosine = jnp.concatenate([jnp.cos(angles), jnp.cos(angles)], axis=1)
    sine_table = jnp.concatenate([jnp.sin(angles), jnp.sin(angles)], axis=1)
    return (cosine, sine_table)


def rotate(heads, cosine, sine_table):
    widened = heads.astype(jnp.float32)
    half_dim = widened.shape[-1] // 2
    turned = jnp.concatenate([-widened[..., half_dim:], widened[..., :half_dim]], axis=-1)
    return (widened * cosine[:, None, :] + turned * sine_table[:, None, :]).astype(jnp.bfloat16)


def rms_norm(row_values, norm_gain):
    widened = row_values.astype(jnp.float32)
    inv_rms = lax.rsqrt(jnp.mean(widened * widened, axis=-1, keepdims=True) + EPSILON)
    return (widened * inv_rms * norm_gain.astype(jnp.float32)).astype(jnp.bfloat16)


def place_rows(values, dest_index, length):
    blank_rows = jnp.zeros((length,) + values.shape[1:], values.dtype)
    return blank_rows.at[dest_index].set(values, mode="drop")


def assemble(first_part, second_part, first_len):
    padded = jnp.concatenate([first_part, jnp.zeros_like(second_part)], axis=0)
    return lax.dynamic_update_slice(padded, second_part, (first_len, jnp.int32(0)))


def attention(projected, total_len, q_heads, kv_heads, head_dim):
    length = projected.shape[0]
    cosine, sine_table = rope_tables(length, head_dim)
    queries = rotate(
        projected[:, : q_heads * head_dim].reshape(length, q_heads, head_dim), cosine, sine_table
    )
    key_heads = rotate(
        projected[:, q_heads * head_dim : (q_heads + kv_heads) * head_dim].reshape(
            length, kv_heads, head_dim
        ),
        cosine,
        sine_table,
    )
    value_heads = projected[:, (q_heads + kv_heads) * head_dim :].reshape(
        length, kv_heads, head_dim
    )
    grouped = queries.reshape(length, kv_heads, q_heads // kv_heads, head_dim)
    block_length = min(BLOCK_ROWS, length)
    root_dim = jnp.sqrt(jnp.float32(head_dim))
    pieces = []
    for row_start in range(0, length, block_length):
        row_stop = row_start + block_length
        scores = (
            jnp.einsum(
                "qkgd,skd->kgqs",
                grouped[row_start:row_stop],
                key_heads[:row_stop],
                preferred_element_type=jnp.float32,
            )
            / root_dim
        )
        row_ids = jnp.arange(row_start, row_stop, dtype=jnp.int32)[:, None]
        col_ids = jnp.arange(row_stop, dtype=jnp.int32)[None, :]
        allowed = (col_ids <= row_ids) & (col_ids < total_len)
        scores = jnp.where(allowed, scores, -jnp.inf)
        largest = jnp.max(scores, axis=-1, keepdims=True)
        exponent = jnp.exp(scores - largest)
        probabilities = (exponent / jnp.sum(exponent, axis=-1, keepdims=True)).astype(jnp.bfloat16)
        mixture = jnp.einsum(
            "kgqs,skd->qkgd",
            probabilities,
            value_heads[:row_stop],
            preferred_element_type=jnp.float32,
        )
        live_rows = (jnp.arange(row_start, row_stop, dtype=jnp.int32) < total_len)[
            :, None, None, None
        ]
        mixture = jnp.where(live_rows, mixture, 0.0)
        pieces.append(mixture.astype(jnp.bfloat16).reshape(block_length, q_heads * head_dim))
    return jnp.concatenate(pieces, axis=0)


def shards(storage, row_doc, row_pos, doc_len, partner, norm_gain, qkv_weight, qkv_bias):
    pair_count = lax.axis_size("pair")
    doc_count = 2 * pair_count
    core = lax.axis_index("core")
    me_index = lax.axis_index("pair") * 2 + core
    half_rows = HALF
    per_dest = half_rows // doc_count
    scorer, own_doc = pairing(partner)
    doc_ids = jnp.arange(doc_count, dtype=jnp.int32)
    first_doc = jnp.sum(jnp.where(doc_ids == me_index, own_doc, 0))
    second_doc = jnp.sum(jnp.where(doc_ids == first_doc, partner, 0))
    first_len = jnp.sum(jnp.where(doc_ids == first_doc, doc_len, 0))
    second_len = jnp.sum(jnp.where(doc_ids == second_doc, doc_len, 0))
    total_len = first_len + second_len
    stored = row_doc >= 0
    dest_scorer = jnp.sum(
        jnp.where(row_doc[:, None] == doc_ids[None, :], scorer[None, :], 0), axis=1
    )
    onehot = ((dest_scorer[:, None] == doc_ids[None, :]) & stored[:, None]).astype(jnp.int32)
    dest_rank = jnp.sum(jnp.cumsum(onehot, axis=0) * onehot, axis=1) - 1
    dest_index = jnp.where(stored, dest_scorer * per_dest + dest_rank, doc_count * per_dest)
    send_rows = place_rows(storage, dest_index, doc_count * per_dest).reshape(
        doc_count, per_dest, storage.shape[1]
    )
    send_pos = (
        jnp.full((doc_count * per_dest,), half_rows, jnp.int32)
        .at[dest_index]
        .set(row_pos, mode="drop")
    )
    send_pos = send_pos.reshape(doc_count, per_dest)
    doc_axes = ("pair", "core")
    got_rows, got_pos = (
        lax.all_to_all(send_rows, doc_axes, split_axis=0, concat_axis=0, tiled=True),
        lax.all_to_all(send_pos, doc_axes, split_axis=0, concat_axis=0, tiled=True),
    )
    own_rows = place_rows(
        got_rows.reshape(doc_count * per_dest, storage.shape[1]), got_pos.reshape(-1), half_rows
    )
    q_heads = HEADS // lax.axis_size("tp")
    kv_heads = KVH // lax.axis_size("tp")
    bias_wide = qkv_bias.astype(jnp.float32)
    own_full = lax.all_gather(own_rows, "tp", axis=1, tiled=True)
    normed = rms_norm(own_full, norm_gain)
    mine = lax.all_gather(qkv_weight, "pair", axis=0, tiled=False)
    theirs = from_partner(mine, "core", 0)
    is_first = core == 0
    low = jnp.where(is_first, mine, theirs)
    high = jnp.where(is_first, theirs, mine)
    full_weight = jnp.stack([low, high], axis=1).reshape(-1, qkv_weight.shape[1])
    own_sum = jnp.dot(normed, full_weight, preferred_element_type=jnp.float32)
    own_proj = (own_sum + bias_wide).astype(jnp.bfloat16)
    other_proj = from_partner(own_proj, "core", 0)
    projected = assemble(own_proj, other_proj, first_len)
    return attention(projected, total_len, q_heads, kv_heads, HD)


def solution(mesh):
    doc_count, tp_count = (mesh.shape["doc"], mesh.shape["tp"])
    split = jax.sharding.Mesh(
        mesh.devices.reshape(doc_count // 2, 2, tp_count), ("pair", "core", "tp")
    )
    rows = ("pair", "core")
    placed = (P(rows, "tp"), P(rows), P(rows), P(), P(), P(), P(rows, "tp"), P("tp"))
    return jax.shard_map(
        shards, mesh=split, in_specs=placed, out_specs=P(rows, "tp"), check_vma=False
    )
```

profile of v0, /device:TPU:1, one launch (start us, length us, event | category | flops | bytes accessed | tf_op | source)
XLA Modules:
  0.0 248.7 jit_solution(14632437046160385297)
XLA Ops:
  14.2 2.6 %scatter_custom_fusion = s32[512]{0:T(512)S(1)} fusion(s32[512]{0:T(512)S(1)} %compare_select_fusion.1, s32[512]{0:T(512)} %param.10, s32[]{:T(128)} %constant.27.clone.1), kind=kCustom, calls=%fused_computation.99 | custom fusion | bytes 2560 | tf_op jit(solution)/shard_map/scatter | solution.py:146
  17.5 13.2 %all-to-all-start = ((s32[64,1,8]{2,1,0:T(1,128)}), s32[64,1,8]{2,1,0:T(1,128)S(1)}, u32[]{:S(2)}, u32[]{:S(2)}) async-start(s32[64,1,8]{2,1,0:T(1,128)} %bitcast.4), calls=%async_computation | async-start | bytes 65536 | tf_op jit(solution)/shard_map/all_to_all | solution.py:152
  30.7 4.3 %scatter_custom_fusion.1 = bf16[512,896]{1,0:T(8,128)(2,1)} fusion(s32[512]{0:T(512)S(1)} %compare_select_fusion.1, bf16[512,896]{1,0:T(8,128)(2,1)} %param.8, bf16[]{:T(256)} %constant.17.clone.1), kind=kCustom, calls=%fused_computation.65 | custom fusion | bytes 918016 | tf_op jit(solution)/shard_map/scatter | solution.py:59
  34.9 5.2 %all-to-all-done = s32[64,1,8]{2,1,0:T(1,128)S(1)} async-done(((s32[64,1,8]{2,1,0:T(1,128)}), s32[64,1,8]{2,1,0:T(1,128)S(1)}, u32[]{:S(2)}, u32[]{:S(2)}) %all-to-all-start) | async-done | bytes 2080 | tf_op jit(solution)/shard_map/all_to_all | solution.py:152
  40.1 5.1 %all-to-all-start.1 = ((bf16[64,8,896]{2,1,0:T(8,128)(2,1)}), bf16[64,8,896]{2,1,0:T(8,128)(2,1)S(1)}, u32[]{:S(2)}, u32[]{:S(2)}) async-start(bf16[64,8,896]{2,1,0:T(8,128)(2,1)} %bitcast.6), calls=%async_computation.1 | async-start | bytes 1835008 | tf_op jit(solution)/shard_map/all_to_all | solution.py:151
  46.7 24.7 %all-to-all-done.1 = bf16[64,8,896]{2,1,0:T(8,128)(2,1)S(1)} async-done(((bf16[64,8,896]{2,1,0:T(8,128)(2,1)}), bf16[64,8,896]{2,1,0:T(8,128)(2,1)S(1)}, u32[]{:S(2)}, u32[]{:S(2)}) %all-to-all-start.1) | async-done | bytes 917536 | tf_op jit(solution)/shard_map/all_to_all | solution.py:151
  71.4 3.6 %scatter_custom_fusion.2 = bf16[512,896]{1,0:T(8,128)(2,1)} fusion(s32[512]{0:T(512)S(1)} %bitcast.119, bf16[64,8,896]{2,1,0:T(8,128)(2,1)S(1)} %all-to-all-done.1, bf16[]{:T(256)} %constant.17.clone.1), kind=kCustom, calls=%fused_computation.49 | custom fusion | bytes 1835010 | tf_op jit(solution)/shard_map/scatter | solution.py:59
  75.0 18.9 %all-gather.6.cloned.1.call-done = bf16[1792,1152]{1,0:T(8,128)(2,1)} async-done(((bf16[56,1152]{1,0:T(8,128)(2,1)}), bf16[1792,1152]{1,0:T(8,128)(2,1)}) %all-gather.6.cloned.1.call-update) | async-done | bytes 4128784 | tf_op jit(solution)/shard_map/all_gather | solution.py:162
  94.0 4.2 %collective-permute-start = (bf16[32,56,1152]{2,1,0:T(8,128)(2,1)}, bf16[32,56,1152]{2,1,0:T(8,128)(2,1)}, u32[]{:S(2)}, u32[]{:S(2)}) collective-permute-start(bf16[32,56,1152]{2,1,0:T(8,128)(2,1)} %bitcast.114), channel_id=1, source_target_pairs={{0,4},{4,0},{1,5},{5,1},{2,6},{6,2},{3,7},{7,3},{8,12},{12,8},{9,1... | collective-permute-start | bytes 12386312 | tf_op jit(solution)/shard_map/ppermute | solution.py:18
  100.4 42.4 %all-gather.4.cloned.1.call-done = bf16[512,3584]{1,0:T(8,128)(2,1)} async-done(((bf16[512,896]{1,0:T(8,128)(2,1)}), bf16[512,3584]{1,0:T(8,128)(2,1)}) %all-gather.4.cloned.1.call-update) | async-done | bytes 3670032 | tf_op jit(solution)/shard_map/all_gather | solution.py:160
  142.8 2.8 %fusion.2 = f32[512]{0:T(512)S(1)} fusion(bf16[512,3584]{1,0:T(8,128)(2,1)} %all-gather.4.cloned.1.call-done), kind=kLoop, calls=%fused_computation.11 | loop fusion | flops 5504512 | bytes 3672064 | tf_op jit(solution)/shard_map/reduce_sum | solution.py:53
  145.6 5.1 %select_bitcast_fusion.1 = (bf16[32,1,56,1152]{3,2,1,0:T(8,128)(2,1)S(1)}, bf16[32,1,56,1152]{3,2,1,0:T(8,128)(2,1)}) fusion(bf16[32,56,1152]{2,1,0:T(8,128)(2,1)} %bitcast.115, bf16[32,56,1152]{2,1,0:T(8,128)(2,1)} %collective-permute-done, pred[]{:T(512)S(6)} %eq.110), kind=kLoop, calls=%fused_computation.22 | loop fusion | flops 4128768 | bytes 16515073 | tf_op jit(solution)/shard_map/stack | solution.py:167
  150.7 6.2 %pad_maximum_fusion = bf16[32,2,56,1152]{3,2,1,0:T(8,128)(2,1)} fusion(bf16[32,1,56,1152]{3,2,1,0:T(8,128)(2,1)} %get-tuple-element.8, bf16[32,1,56,1152]{3,2,1,0:T(8,128)(2,1)S(1)} %get-tuple-element.7), kind=kLoop, calls=%fused_computation.10 | loop fusion | flops 4128768 | bytes 16515072 | tf_op jit(solution)/shard_map/stack | solution.py:167
  156.9 10.4 %fusion.21 = bf16[512,1152]{1,0:T(8,128)(2,1)} fusion(bf16[3584,1152]{1,0:T(8,128)(2,1)} %bitcast.113, bf16[512,3584]{1,0:T(8,128)(2,1)} %all-gather.4.cloned.1.call-done, f32[3584]{0:T(1024)S(1)} %convert_element_type.65, f32[512]{0:T(512)S(1)} %add_rsqrt_fusion, f32[1152]{0:T(1024)S(1)} %convert_element_type.67), kind=kOutput, calls=%fused_computation.34 | convolution fusion | flops 4236378112 | bytes 13128192 | tf_op jit(solution)/shard_map/dot_general | solution.py:168
  173.7 2.8 %fusion.42 = (f32[1024,64]{1,0:T(8,128)}, f32[1024,64]{1,0:T(8,128)}) fusion(f32[64]{0:T(128)S(1)} %multiply_exponential_fusion), kind=kLoop, calls=%fused_computation.63 | loop fusion | flops 65536 | bytes 524544 | tf_op jit(solution)/shard_map/cos | solution.py:39
  178.0 7.4 %dynamic_update_slice.3 = bf16[1024,1152]{1,0:T(8,128)(2,1)S(1)} dynamic-update-slice(bf16[1024,1152]{1,0:T(8,128)(2,1)S(1)} %concatenate.23, bf16[512,1152]{1,0:T(8,128)(2,1)} %collective-permute-done.1, s32[]{:T(128)S(6)} %select_n.78, s32[]{:T(128)} %constant.24.clone.1) | dynamic-update-slice | bytes 2359300 | tf_op jit(solution)/shard_map/dynamic_update_slice | solution.py:64
  185.5 2.2 slice_convert_fusion
  188.9 5.0 %copy.50 = f32[1024,896]{0,1:T(8,128)} copy(f32[1024,896]{1,0:T(8,128)} %slice_convert_fusion) | data formatting | bytes 7340032 | tf_op jit(solution)/shard_map/convert_element_type | solution.py:45
  193.9 5.0 %copy.51 = f32[1024,7,128]{2,0,1:T(8,128)} copy(f32[1024,7,128]{0,2,1:T(8,128)} %bitcast.112) | data formatting | bytes 7340032 | tf_op jit(solution)/shard_map/convert_element_type | solution.py:45
  199.0 4.5 %slice_negate_fusion = (f32[1024,7,64]{2,0,1:T(8,128)S(1)}, f32[1024,7,64]{2,0,1:T(8,128)S(1)}) fusion(f32[1024,7,128]{2,0,1:T(8,128)} %copy.51), kind=kLoop, calls=%fused_computation.24 | loop fusion | flops 458752 | bytes 7340032 | tf_op jit(solution)/shard_map/neg | solution.py:47
  209.4 4.0 %fusion.26 = bf16[1,128,7,512]{3,1,2,0:T(8,128)(2,1)} fusion(f32[7,512]{1,0:T(8,128)S(1)} %fusion.7, f32[7,512]{1,0:T(8,128)S(1)} %get-tuple-element.22, f32[512,512,7]{1,0,2:T(8,128)S(1)} %get-tuple-element.23, pred[512,512]{0,1:T(8,128)(4,1)S(1)} %fusion.31, pred[512]{0:T(512)(128)(4,1)S(1)} %get-tuple-element.24, bf16[1024,1152]{1,0:T(8,128)(2,1)} %copy-done.1), kind=kOutput, calls=%fused_computation.42 | convolution fusion | flops 479854592 | bytes 8679936 | tf_op jit(solution)/shard_map/kgqs,skd->qkgd/dot_general | solution.py:105
  215.7 6.5 %fusion.1 = (f32[7,512]{1,0:T(8,128)S(1)}, f32[1024,512,7]{1,0,2:T(8,128)}) fusion(pred[512,1024]{0,1:T(8,128)(4,1)S(1)} %fusion.24, bf16[1024,7,128]{2,0,1:T(8,128)(2,1)S(1)} %fusion.12, bf16[1024,128]{1,0:T(8,128)(2,1)S(1)} %get-tuple-element.11), kind=kOutput, calls=%fused_computation.7 | convolution fusion | flops 950530560 | bytes 16398336 | tf_op jit(solution)/shard_map/qkgd,skd->kgqs/dot_general | solution.py:90
  222.2 8.2 %fusion = f32[7,512]{1,0:T(8,128)S(1)} fusion(f32[1024,512,7]{1,0,2:T(8,128)} %get-tuple-element.21, f32[7,512]{1,0:T(8,128)S(1)} %get-tuple-element.20, pred[512,1024]{0,1:T(8,128)(4,1)S(1)} %fusion.24), kind=kLoop, calls=%fused_computation.6 | loop fusion | flops 14676480 | bytes 15233024 | tf_op jit(solution)/shard_map/reduce_sum | solution.py:104
  230.4 8.5 %fusion.25 = bf16[1,128,7,512]{3,1,2,0:T(8,128)(2,1)} fusion(f32[7,512]{1,0:T(8,128)S(1)} %fusion, f32[7,512]{1,0:T(8,128)S(1)} %get-tuple-element.20, f32[1024,512,7]{1,0,2:T(8,128)} %get-tuple-element.21, pred[512,1024]{0,1:T(8,128)(4,1)S(1)} %fusion.24, pred[512]{0:T(512)(128)(4,1)S(1)} %get-tuple-element.25, bf16[1024,1152]{1,0:T(8,128)(2,1)} %copy-done.1), kind=kOutput, calls=%fused_computation.40 | convolution fusion | flops 958791680 | bytes 16413184 | tf_op jit(solution)/shard_map/kgqs,skd->qkgd/dot_general | solution.py:105
  (74 shorter events, 28.9 us)
Async XLA Ops:
  6.5 92.5 %copy-start.10 = (s32[64]{0:T(128)S(1)}, s32[64]{0:T(128)}, u32[]{:S(2)}) copy-start(s32[64]{0:T(128)} %param.12) | copy-start | bytes 772
  6.5 91.7 %copy-start.7 = (bf16[3584]{0:T(1024)(128)(2,1)S(1)}, bf16[3584]{0:T(1024)(128)(2,1)}, u32[]{:S(2)}) copy-start(bf16[3584]{0:T(1024)(128)(2,1)} %param.13) | copy-start | bytes 21508
  6.5 91.7 %copy-start.8 = (bf16[1152]{0:T(1024)(128)(2,1)S(1)}, bf16[1152]{0:T(1024)(128)(2,1)}, u32[]{:S(2)}) copy-start(bf16[1152]{0:T(1024)(128)(2,1)} %param.15) | copy-start | bytes 6916
  6.5 87.4 %all-gather.6.cloned.1.call-start = ((), (), s32[]{:S(2)}) async-start(), calls=%async_computation.3 | async-start | bytes 4257792 | tf_op jit(solution)/shard_map/all_gather | solution.py:162
  17.5 22.6 %all-to-all-start = ((s32[64,1,8]{2,1,0:T(1,128)}), s32[64,1,8]{2,1,0:T(1,128)S(1)}, u32[]{:S(2)}, u32[]{:S(2)}) async-start(s32[64,1,8]{2,1,0:T(1,128)} %bitcast.4), calls=%async_computation | async-start | bytes 65536 | tf_op jit(solution)/shard_map/all_to_all | solution.py:152
  40.1 31.3 %all-to-all-start.1 = ((bf16[64,8,896]{2,1,0:T(8,128)(2,1)}), bf16[64,8,896]{2,1,0:T(8,128)(2,1)S(1)}, u32[]{:S(2)}, u32[]{:S(2)}) async-start(bf16[64,8,896]{2,1,0:T(8,128)(2,1)} %bitcast.6), calls=%async_computation.1 | async-start | bytes 1835008 | tf_op jit(solution)/shard_map/all_to_all | solution.py:151
  45.2 97.5 %all-gather.4.cloned.1.call-start = ((), (), s32[]{:S(2)}) async-start(), calls=%async_computation.2 | async-start | bytes 4587520 | tf_op jit(solution)/shard_map/all_gather | solution.py:160
  94.0 51.6 %collective-permute-start = (bf16[32,56,1152]{2,1,0:T(8,128)(2,1)}, bf16[32,56,1152]{2,1,0:T(8,128)(2,1)}, u32[]{:S(2)}, u32[]{:S(2)}) collective-permute-start(bf16[32,56,1152]{2,1,0:T(8,128)(2,1)} %bitcast.114), channel_id=1, source_target_pairs={{0,4},{4,0},{1,5},{5,1},{2,6},{6,2},{3,7},{7,3},{8,12},{12,8},{9,1... | collective-permute-start | bytes 12386312 | tf_op jit(solution)/shard_map/ppermute | solution.py:18
  156.9 11.2 %copy-start.9 = (s32[64]{0:T(128)S(1)}, s32[64]{0:T(128)}, u32[]{:S(2)}) copy-start(s32[64]{0:T(128)} %param.11) | copy-start | bytes 772
  167.3 10.7 %collective-permute-start.1 = (bf16[512,1152]{1,0:T(8,128)(2,1)}, bf16[512,1152]{1,0:T(8,128)(2,1)}, u32[]{:S(2)}, u32[]{:S(2)}) collective-permute-start(bf16[512,1152]{1,0:T(8,128)(2,1)} %fusion.21), channel_id=1, source_target_pairs={{0,4},{4,0},{1,5},{5,1},{2,6},{6,2},{3,7},{7,3},{8,12},{12,8},{9,1... | collective-permute-start | bytes 3538952 | tf_op jit(solution)/shard_map/ppermute | solution.py:18
  185.5 18.0 %copy-start.1 = (bf16[1024,1152]{1,0:T(8,128)(2,1)}, bf16[1024,1152]{1,0:T(8,128)(2,1)S(1)}, u32[]{:S(2)}) copy-start(bf16[1024,1152]{1,0:T(8,128)(2,1)S(1)} %dynamic_update_slice.3) | copy-start | bytes 7077892
  199.0 4.5 %copy-start.3 = (f32[1024,64]{1,0:T(8,128)S(1)}, f32[1024,64]{1,0:T(8,128)}, u32[]{:S(2)}) copy-start(f32[1024,64]{1,0:T(8,128)} %get-tuple-element.16) | copy-start | bytes 786436
  199.0 4.5 %copy-start.4 = (f32[1024,64]{1,0:T(8,128)S(1)}, f32[1024,64]{1,0:T(8,128)}, u32[]{:S(2)}) copy-start(f32[1024,64]{1,0:T(8,128)} %get-tuple-element.17) | copy-start | bytes 786436
  199.0 4.5 %copy-start.5 = (f32[1024,64]{1,0:T(8,128)S(1)}, f32[1024,64]{1,0:T(8,128)}, u32[]{:S(2)}) copy-start(f32[1024,64]{1,0:T(8,128)} %get-tuple-element.14) | copy-start | bytes 786436
  199.0 4.5 %copy-start.6 = (f32[1024,64]{1,0:T(8,128)S(1)}, f32[1024,64]{1,0:T(8,128)}, u32[]{:S(2)}) copy-start(f32[1024,64]{1,0:T(8,128)} %get-tuple-element.15) | copy-start | bytes 786436
  203.5 2.0 copy-start
  230.4 10.1 %copy-start.2 = (bf16[512,896]{1,0:T(8,128)(2,1)S(1)}, bf16[512,896]{1,0:T(8,128)(2,1)}, u32[]{:S(2)}) copy-start(bf16[512,896]{1,0:T(8,128)(2,1)} %copy.58) | copy-start | bytes 2752516
Sparse Core Ops, SparseCore 0:
  10.0 83.9 all-gather.5
  95.8 46.9 all-gather.3
where the time goes:
time: 250 us; the launch traced here: 249 us
  waiting for transfers between devices  91.9 us (37%)
  other arithmetic  49.6 us (20%)
  local copies, waits for them, and re-layouts  36.4 us (15%)
  matrix products  30.8 us (12%)
  starting transfers between devices  23.3 us (9%)
  between operations  16.8 us (7%)
    all_gather x1, waiting for transfers between devices, shards(): own_full = lax.all_gather(own_rows, 'tp', axis=1, tiled=True)  42.4 us
    all_to_all x1, waiting for transfers between devices, shards(): lax.all_to_all(send_rows, doc_axes, split_axis=0, concat_axis=0, tiled=True)  24.7 us
    all_gather x1, waiting for transfers between devices, shards(): mine = lax.all_gather(qkv_weight, 'pair', axis=0, tiled=False)  18.9 us
    all_to_all x1, starting transfers between devices, shards(): lax.all_to_all(send_pos, doc_axes, split_axis=0, concat_axis=0, tiled=True)  13.2 us
    dot_general x2, matrix products, attention(): jnp.einsum('kgqs,skd->qkgd', probabilities, value_heads[:row_stop], prefe...  12.6 us
    another operation x2, other arithmetic, shards(): jnp.stack([low, high], axis=1).reshape(-1, qkv_weight.shape[1])  11.3 us
    dot_general x1, matrix products, shards(): own_sum = jnp.dot(normed, full_weight, preferred_element_type=jnp.float32)  10.4 us
    convert_element_type x2, local copies, waits for them, and re-layouts, rotate(): widened = heads.astype(jnp.float32)  10.1 us
  transfers between devices with their start and end apart: 6, of which 4 were waited for; matrix products, arithmetic and copies ran while one was open for 12% of the time, Pallas kernels for 0%

commit v1 on v0

--- a/solution.py
+++ b/solution.py
@@ -157,7 +157,10 @@
     q_heads = HEADS // lax.axis_size("tp")
     kv_heads = KVH // lax.axis_size("tp")
     bias_wide = qkv_bias.astype(jnp.float32)
-    own_full = lax.all_gather(own_rows, "tp", axis=1, tiled=True)
+    size = lax.axis_size("tp")
+    shards_2 = jnp.stack([own_rows for _ in range(size)])
+    shards_2 = lax.all_to_all(shards_2, "tp", split_axis=0, concat_axis=0)
+    own_full = jnp.concatenate(shards_2, axis=1)
     normed = rms_norm(own_full, norm_gain)
     mine = lax.all_gather(qkv_weight, "pair", axis=0, tiled=False)
     theirs = from_partner(mine, "core", 0)

time: 250 us -> 264 us (1.056)
  starting transfers between devices: 23.3 us -> 28.6 us
  waiting for transfers between devices: 91.9 us -> 95.6 us
  other arithmetic: 49.6 us -> 52.4 us
    all_gather x1 -> x0, waiting for transfers between devices: 42.4 us -> none  [shards(): own_full = lax.all_gather(own_rows, 'tp', axis=1, tiled=True)]
    all_to_all x0 -> x1, waiting for transfers between devices: none -> 41 us  [shards(): shards_2 = lax.all_to_all(shards_2, 'tp', split_axis=0, concat_axis=0)]
    all_gather x1, waiting for transfers between devices: 18.9 us -> 48.7 us  [shards(): mine = lax.all_gather(qkv_weight, 'pair', axis=0, tiled=False)]
    all_to_all x1, waiting for transfers between devices: 24.7 us -> 0.01 us  [shards(): lax.all_to_all(send_rows, doc_axes, split_axis=0, concat_axis=0, tiled=True)]
    all_to_all x0 -> x1, starting transfers between devices: none -> 5.11 us  [shards(): shards_2 = lax.all_to_all(shards_2, 'tp', split_axis=0, concat_axis=0)]
    convert_element_type x1, other arithmetic: 0.01 us -> 3.95 us  [rms_norm(): (widened * inv_rms * norm_gain.astype(jnp.float32)).astype(jnp.bfloat16)]
    scatter x2 -> x3, local copies, waits for them, and re-layouts: 7.91 us -> 7.74 us  [place_rows(): return blank_rows.at[dest_index].set(values, mode='drop')]
  transfers between devices with their start and end apart: 6 -> 6, of which waited for: 4 -> 3; matrix products, arithmetic and copies ran while one was open for 12% -> 14% of each run, Pallas kernels for 0% -> 0%
where the time goes in v1:
time: 264 us; the launch traced here: 262 us
  waiting for transfers between devices  95.6 us (36%)
  other arithmetic  52.4 us (20%)
  local copies, waits for them, and re-layouts  38.3 us (15%)
  matrix products  30.8 us (12%)
  starting transfers between devices  28.6 us (11%)
  between operations  16.8 us (6%)
    all_gather x1, waiting for transfers between devices, shards(): mine = lax.all_gather(qkv_weight, 'pair', axis=0, tiled=False)  48.7 us
    all_to_all x1, waiting for transfers between devices, shards(): shards_2 = lax.all_to_all(shards_2, 'tp', split_axis=0, concat_axis=0)  41 us
    all_to_all x1, starting transfers between devices, shards(): lax.all_to_all(send_pos, doc_axes, split_axis=0, concat_axis=0, tiled=True)  13.2 us
    dot_general x2, matrix products, attention(): jnp.einsum('kgqs,skd->qkgd', probabilities, value_heads[:row_stop], prefe...  12.6 us
    dot_general x1, matrix products, shards(): own_sum = jnp.dot(normed, full_weight, preferred_element_type=jnp.float32)  10.4 us
    another operation x2, other arithmetic, shards(): jnp.stack([low, high], axis=1).reshape(-1, qkv_weight.shape[1])  10.1 us
    convert_element_type x2, local copies, waits for them, and re-layouts, rotate(): widened = heads.astype(jnp.float32)  10.1 us
    reduce_sum x2, other arithmetic, attention(): jnp.sum(exponent, axis=-1, keepdims=True)  9.7 us
  transfers between devices with their start and end apart: 6, of which 3 were waited for; matrix products, arithmetic and copies ran while one was open for 14% of the time, Pallas kernels for 0%

profile of v1, /device:TPU:1, one launch (start us, length us, event | category | flops | bytes accessed | tf_op | source)
XLA Modules:
  0.0 262.5 jit_solution(10474192305787739962)
XLA Ops:
  14.2 2.6 scatter_custom_fusion
  17.5 13.2 %all-to-all-start = ((s32[64,1,8]{2,1,0:T(1,128)}), s32[64,1,8]{2,1,0:T(1,128)S(1)}, u32[]{:S(2)}, u32[]{:S(2)}) async-start(s32[64,1,8]{2,1,0:T(1,128)} %bitcast.4), calls=%async_computation | async-start | bytes 65536 | tf_op jit(solution)/shard_map/all_to_all | solution.py:152
  30.7 4.3 %scatter_custom_fusion.1 = bf16[512,896]{1,0:T(8,128)(2,1)} fusion(s32[512]{0:T(512)S(1)} %compare_select_fusion.1, bf16[512,896]{1,0:T(8,128)(2,1)} %param.8, bf16[]{:T(256)} %constant.17.clone.1), kind=kCustom, calls=%fused_computation.62 | custom fusion | bytes 918016 | tf_op jit(solution)/shard_map/scatter | solution.py:59
  34.9 5.2 %all-to-all-done = s32[64,1,8]{2,1,0:T(1,128)S(1)} async-done(((s32[64,1,8]{2,1,0:T(1,128)}), s32[64,1,8]{2,1,0:T(1,128)S(1)}, u32[]{:S(2)}, u32[]{:S(2)}) %all-to-all-start) | async-done | bytes 2080 | tf_op jit(solution)/shard_map/all_to_all | solution.py:152
  40.1 5.1 %all-to-all-start.1 = ((bf16[64,8,896]{2,1,0:T(8,128)(2,1)}), bf16[64,8,896]{2,1,0:T(8,128)(2,1)S(1)}, u32[]{:S(2)}, u32[]{:S(2)}) async-start(bf16[64,8,896]{2,1,0:T(8,128)(2,1)} %bitcast.6), calls=%async_computation.1 | async-start | bytes 1835008 | tf_op jit(solution)/shard_map/all_to_all | solution.py:151
  45.2 48.7 %all-gather.3.cloned.1.call-done = bf16[1792,1152]{1,0:T(8,128)(2,1)} async-done(((bf16[56,1152]{1,0:T(8,128)(2,1)}), bf16[1792,1152]{1,0:T(8,128)(2,1)}) %all-gather.3.cloned.1.call-update) | async-done | bytes 4128784 | tf_op jit(solution)/shard_map/all_gather | solution.py:165
  94.0 4.4 %collective-permute-start = (bf16[32,56,1152]{2,1,0:T(8,128)(2,1)}, bf16[32,56,1152]{2,1,0:T(8,128)(2,1)}, u32[]{:S(2)}, u32[]{:S(2)}) collective-permute-start(bf16[32,56,1152]{2,1,0:T(8,128)(2,1)} %bitcast.118), channel_id=1, source_target_pairs={{0,4},{4,0},{1,5},{5,1},{2,6},{6,2},{3,7},{7,3},{8,12},{12,8},{9,1... | collective-permute-start | bytes 12386312 | tf_op jit(solution)/shard_map/ppermute | solution.py:18
  99.6 2.9 %scatter_custom_fusion.2 = bf16[512,896]{1,0:T(8,128)(2,1)S(1)} fusion(s32[512]{0:T(512)S(1)} %bitcast.124, bf16[64,8,896]{2,1,0:T(8,128)(2,1)S(1)} %all-to-all-done.1, bf16[]{:T(256)} %constant.17.clone.1), kind=kCustom, calls=%fused_computation.46 | custom fusion | bytes 1835010 | tf_op jit(solution)/shard_map/scatter | solution.py:59
  105.3 5.1 %all-to-all-start.2 = ((bf16[4,512,896]{1,2,0:T(8,128)(2,1)}), bf16[4,512,896]{1,2,0:T(8,128)(2,1)}, u32[]{:S(2)}, u32[]{:S(2)}) async-start(bf16[4,512,896]{1,2,0:T(8,128)(2,1)} %stack.16), calls=%async_computation.2 | async-start | bytes 7340032 | tf_op jit(solution)/shard_map/all_to_all | solution.py:162
  112.6 41.0 %all-to-all-done.2 = bf16[4,512,896]{1,2,0:T(8,128)(2,1)} async-done(((bf16[4,512,896]{1,2,0:T(8,128)(2,1)}), bf16[4,512,896]{1,2,0:T(8,128)(2,1)}, u32[]{:S(2)}, u32[]{:S(2)}) %all-to-all-start.2) | async-done | bytes 3670048 | tf_op jit(solution)/shard_map/all_to_all | solution.py:162
  153.6 2.9 %fusion.2 = f32[512]{0:T(512)S(1)} fusion(bf16[4,512,896]{1,2,0:T(8,128)(2,1)} %all-to-all-done.2), kind=kLoop, calls=%fused_computation.11 | loop fusion | flops 5504512 | bytes 3672064 | tf_op jit(solution)/shard_map/reduce_sum | solution.py:53
  156.5 4.0 %fusion.4 = bf16[4,512,896]{1,2,0:T(8,128)(2,1)} fusion(bf16[4,512,896]{1,2,0:T(8,128)(2,1)} %all-to-all-done.2, f32[4,896]{1,0:T(4,128)S(1)} %reshape.238, f32[512]{0:T(512)S(1)} %add_rsqrt_fusion), kind=kLoop, calls=%fused_computation.13 | loop fusion | flops 7340032 | bytes 7356416 | tf_op jit(solution)/shard_map/convert_element_type | solution.py:54
  160.5 3.9 %select_bitcast_fusion.1 = (bf16[32,1,56,1152]{3,2,1,0:T(8,128)(2,1)S(1)}, bf16[32,1,56,1152]{3,2,1,0:T(8,128)(2,1)}) fusion(bf16[32,56,1152]{2,1,0:T(8,128)(2,1)S(1)} %bitcast.119, bf16[32,56,1152]{2,1,0:T(8,128)(2,1)} %collective-permute-done, pred[]{:T(512)S(6)} %eq.110), kind=kLoop, calls=%fused_computation.22 | loop fusion | flops 4128768 | bytes 16515073 | tf_op jit(solution)/shard_map/stack | solution.py:170
  164.4 6.2 %pad_maximum_fusion = bf16[32,2,56,1152]{3,2,1,0:T(8,128)(2,1)} fusion(bf16[32,1,56,1152]{3,2,1,0:T(8,128)(2,1)} %get-tuple-element.8, bf16[32,1,56,1152]{3,2,1,0:T(8,128)(2,1)S(1)} %get-tuple-element.7), kind=kLoop, calls=%fused_computation.10 | loop fusion | flops 4128768 | bytes 16515072 | tf_op jit(solution)/shard_map/stack | solution.py:170
  170.6 10.4 %fusion.14 = bf16[512,1152]{1,0:T(8,128)(2,1)} fusion(bf16[512,3584]{0,1:T(8,128)(2,1)} %bitcast.120, bf16[3584,1152]{1,0:T(8,128)(2,1)} %bitcast.117, f32[1152]{0:T(1024)S(1)} %convert_element_type.75), kind=kOutput, calls=%fused_computation.31 | convolution fusion | flops 4229038080 | bytes 13111808 | tf_op jit(solution)/shard_map/dot_general | solution.py:171
  187.5 2.8 %fusion.33 = (f32[1024,64]{1,0:T(8,128)}, f32[1024,64]{1,0:T(8,128)}) fusion(f32[64]{0:T(128)S(1)} %multiply_exponential_fusion), kind=kLoop, calls=%fused_computation.60 | loop fusion | flops 65536 | bytes 524544 | tf_op jit(solution)/shard_map/cos | solution.py:39
  191.8 7.4 %dynamic_update_slice.3 = bf16[1024,1152]{1,0:T(8,128)(2,1)S(1)} dynamic-update-slice(bf16[1024,1152]{1,0:T(8,128)(2,1)S(1)} %concatenate.23, bf16[512,1152]{1,0:T(8,128)(2,1)} %collective-permute-done.1, s32[]{:T(128)S(6)} %select_n.78, s32[]{:T(128)} %constant.24.clone.1) | dynamic-update-slice | bytes 2359300 | tf_op jit(solution)/shard_map/dynamic_update_slice | solution.py:64
  202.7 5.0 %copy.53 = f32[1024,896]{0,1:T(8,128)} copy(f32[1024,896]{1,0:T(8,128)} %slice_convert_fusion) | data formatting | bytes 7340032 | tf_op jit(solution)/shard_map/convert_element_type | solution.py:45
  207.7 5.0 %copy.54 = f32[1024,7,128]{2,0,1:T(8,128)} copy(f32[1024,7,128]{0,2,1:T(8,128)} %bitcast.116) | data formatting | bytes 7340032 | tf_op jit(solution)/shard_map/convert_element_type | solution.py:45
  212.8 4.5 %slice_negate_fusion = (f32[1024,7,64]{2,0,1:T(8,128)S(1)}, f32[1024,7,64]{2,0,1:T(8,128)S(1)}) fusion(f32[1024,7,128]{2,0,1:T(8,128)} %copy.54), kind=kLoop, calls=%fused_computation.23 | loop fusion | flops 458752 | bytes 7340032 | tf_op jit(solution)/shard_map/neg | solution.py:47
  223.2 4.0 %fusion.17 = bf16[1,128,7,512]{3,1,2,0:T(8,128)(2,1)} fusion(f32[7,512]{1,0:T(8,128)S(1)} %fusion.7, f32[7,512]{1,0:T(8,128)S(1)} %get-tuple-element.22, f32[512,512,7]{1,0,2:T(8,128)S(1)} %get-tuple-element.23, pred[512,512]{0,1:T(8,128)(4,1)S(1)} %fusion.22, pred[512]{0:T(512)(128)(4,1)S(1)} %get-tuple-element.24, bf16[1024,1152]{1,0:T(8,128)(2,1)} %copy-done.1), kind=kOutput, calls=%fused_computation.39 | convolution fusion | flops 479854592 | bytes 8679936 | tf_op jit(solution)/shard_map/kgqs,skd->qkgd/dot_general | solution.py:105
  229.5 6.5 %fusion.1 = (f32[7,512]{1,0:T(8,128)S(1)}, f32[1024,512,7]{1,0,2:T(8,128)}) fusion(pred[512,1024]{0,1:T(8,128)(4,1)S(1)} %fusion.15, bf16[1024,7,128]{2,0,1:T(8,128)(2,1)S(1)} %fusion.10, bf16[1024,128]{1,0:T(8,128)(2,1)S(1)} %get-tuple-element.11), kind=kOutput, calls=%fused_computation.7 | convolution fusion | flops 950530560 | bytes 16398336 | tf_op jit(solution)/shard_map/qkgd,skd->kgqs/dot_general | solution.py:90
  236.0 8.2 %fusion = f32[7,512]{1,0:T(8,128)S(1)} fusion(f32[1024,512,7]{1,0,2:T(8,128)} %get-tuple-element.21, f32[7,512]{1,0:T(8,128)S(1)} %get-tuple-element.20, pred[512,1024]{0,1:T(8,128)(4,1)S(1)} %fusion.15), kind=kLoop, calls=%fused_computation.6 | loop fusion | flops 14676480 | bytes 15233024 | tf_op jit(solution)/shard_map/reduce_sum | solution.py:104
  244.2 8.5 %fusion.16 = bf16[1,128,7,512]{3,1,2,0:T(8,128)(2,1)} fusion(f32[7,512]{1,0:T(8,128)S(1)} %fusion, f32[7,512]{1,0:T(8,128)S(1)} %get-tuple-element.20, f32[1024,512,7]{1,0,2:T(8,128)} %get-tuple-element.21, pred[512,1024]{0,1:T(8,128)(4,1)S(1)} %fusion.15, pred[512]{0:T(512)(128)(4,1)S(1)} %get-tuple-element.25, bf16[1024,1152]{1,0:T(8,128)(2,1)} %copy-done.1), kind=kOutput, calls=%fused_computation.37 | convolution fusion | flops 958791680 | bytes 16413184 | tf_op jit(solution)/shard_map/kgqs,skd->qkgd/dot_general | solution.py:105
  (78 shorter events, 33.7 us)
Async XLA Ops:
  6.5 87.4 %all-gather.3.cloned.1.call-start = ((), (), s32[]{:S(2)}) async-start(), calls=%async_computation.3 | async-start | bytes 4257792 | tf_op jit(solution)/shard_map/all_gather | solution.py:165
  17.5 22.6 %all-to-all-start = ((s32[64,1,8]{2,1,0:T(1,128)}), s32[64,1,8]{2,1,0:T(1,128)S(1)}, u32[]{:S(2)}, u32[]{:S(2)}) async-start(s32[64,1,8]{2,1,0:T(1,128)} %bitcast.4), calls=%async_computation | async-start | bytes 65536 | tf_op jit(solution)/shard_map/all_to_all | solution.py:152
  40.1 59.5 %all-to-all-start.1 = ((bf16[64,8,896]{2,1,0:T(8,128)(2,1)}), bf16[64,8,896]{2,1,0:T(8,128)(2,1)S(1)}, u32[]{:S(2)}, u32[]{:S(2)}) async-start(bf16[64,8,896]{2,1,0:T(8,128)(2,1)} %bitcast.6), calls=%async_computation.1 | async-start | bytes 1835008 | tf_op jit(solution)/shard_map/all_to_all | solution.py:151
  94.0 66.5 %collective-permute-start = (bf16[32,56,1152]{2,1,0:T(8,128)(2,1)}, bf16[32,56,1152]{2,1,0:T(8,128)(2,1)}, u32[]{:S(2)}, u32[]{:S(2)}) collective-permute-start(bf16[32,56,1152]{2,1,0:T(8,128)(2,1)} %bitcast.118), channel_id=1, source_target_pairs={{0,4},{4,0},{1,5},{5,1},{2,6},{6,2},{3,7},{7,3},{8,12},{12,8},{9,1... | collective-permute-start | bytes 12386312 | tf_op jit(solution)/shard_map/ppermute | solution.py:18
  105.3 5.1 %copy-start.8 = (bf16[3584]{0:T(1024)(128)(2,1)S(1)}, bf16[3584]{0:T(1024)(128)(2,1)}, u32[]{:S(2)}) copy-start(bf16[3584]{0:T(1024)(128)(2,1)} %param.13) | copy-start | bytes 21508
  105.3 5.2 %copy-start.9 = (bf16[1152]{0:T(1024)(128)(2,1)S(1)}, bf16[1152]{0:T(1024)(128)(2,1)}, u32[]{:S(2)}) copy-start(bf16[1152]{0:T(1024)(128)(2,1)} %param.15) | copy-start | bytes 6916
  105.3 6.0 %copy-start.11 = (s32[64]{0:T(128)S(1)}, s32[64]{0:T(128)}, u32[]{:S(2)}) copy-start(s32[64]{0:T(128)} %param.12) | copy-start | bytes 772
  105.3 48.4 %all-to-all-start.2 = ((bf16[4,512,896]{1,2,0:T(8,128)(2,1)}), bf16[4,512,896]{1,2,0:T(8,128)(2,1)}, u32[]{:S(2)}, u32[]{:S(2)}) async-start(bf16[4,512,896]{1,2,0:T(8,128)(2,1)} %stack.16), calls=%async_computation.2 | async-start | bytes 7340032 | tf_op jit(solution)/shard_map/all_to_all | solution.py:162
  156.5 4.0 %copy-start.2 = (bf16[1792,1152]{1,0:T(8,128)(2,1)S(1)}, bf16[1792,1152]{1,0:T(8,128)(2,1)}, u32[]{:S(2)}) copy-start(bf16[1792,1152]{1,0:T(8,128)(2,1)} %all-gather.3.cloned.1.call-done) | copy-start | bytes 12386308
  170.6 11.2 %copy-start.10 = (s32[64]{0:T(128)S(1)}, s32[64]{0:T(128)}, u32[]{:S(2)}) copy-start(s32[64]{0:T(128)} %param.11) | copy-start | bytes 772
  181.0 10.8 %collective-permute-start.1 = (bf16[512,1152]{1,0:T(8,128)(2,1)}, bf16[512,1152]{1,0:T(8,128)(2,1)}, u32[]{:S(2)}, u32[]{:S(2)}) collective-permute-start(bf16[512,1152]{1,0:T(8,128)(2,1)} %fusion.14), channel_id=1, source_target_pairs={{0,4},{4,0},{1,5},{5,1},{2,6},{6,2},{3,7},{7,3},{8,12},{12,8},{9,1... | collective-permute-start | bytes 3538952 | tf_op jit(solution)/shard_map/ppermute | solution.py:18
  199.2 18.0 %copy-start.1 = (bf16[1024,1152]{1,0:T(8,128)(2,1)}, bf16[1024,1152]{1,0:T(8,128)(2,1)S(1)}, u32[]{:S(2)}) copy-start(bf16[1024,1152]{1,0:T(8,128)(2,1)S(1)} %dynamic_update_slice.3) | copy-start | bytes 7077892
  212.7 4.5 %copy-start.4 = (f32[1024,64]{1,0:T(8,128)S(1)}, f32[1024,64]{1,0:T(8,128)}, u32[]{:S(2)}) copy-start(f32[1024,64]{1,0:T(8,128)} %get-tuple-element.16) | copy-start | bytes 786436
  212.7 4.5 %copy-start.5 = (f32[1024,64]{1,0:T(8,128)S(1)}, f32[1024,64]{1,0:T(8,128)}, u32[]{:S(2)}) copy-start(f32[1024,64]{1,0:T(8,128)} %get-tuple-element.17) | copy-start | bytes 786436
  212.7 4.5 %copy-start.6 = (f32[1024,64]{1,0:T(8,128)S(1)}, f32[1024,64]{1,0:T(8,128)}, u32[]{:S(2)}) copy-start(f32[1024,64]{1,0:T(8,128)} %get-tuple-element.14) | copy-start | bytes 786436
  212.7 4.5 %copy-start.7 = (f32[1024,64]{1,0:T(8,128)S(1)}, f32[1024,64]{1,0:T(8,128)}, u32[]{:S(2)}) copy-start(f32[1024,64]{1,0:T(8,128)} %get-tuple-element.15) | copy-start | bytes 786436
  217.2 2.0 copy-start
  244.2 10.1 %copy-start.3 = (bf16[512,896]{1,0:T(8,128)(2,1)S(1)}, bf16[512,896]{1,0:T(8,128)(2,1)}, u32[]{:S(2)}) copy-start(bf16[512,896]{1,0:T(8,128)(2,1)} %copy.61) | copy-start | bytes 2752516
Sparse Core Ops, SparseCore 0:
  10.0 83.9 all-gather.2
